TPU v7x, 32 devices: a whole 2x2x4 slice. The times are simulated.
32 devices in a mesh: tm: 2 (over core), height: 16 (over z, y, x).
Axes of the slice: x: 2, y: 2, z: 4, core: 2. Of those that a mesh axis runs over, the one named last changes fastest.
Arguments:
- clip: bfloat16 [4, 128, 48, 256], P('tm', 'height'), may hold values from -6 to 6
- teacher: bfloat16 [4, 128, 48, 256], P('tm', 'height'), may hold values from -6 to 6
- kernel_one: bfloat16 [6912, 256], P('height'), may hold values from -0.078125 to 0.078125
- kernel_two: bfloat16 [6912, 256], P('height'), may hold values from -0.078125 to 0.078125
Outputs:
- student: bfloat16 [4, 128, 48, 256], P('tm', 'height')
- grad_one: float32 [6912, 256], P('height')
- grad_two: float32 [6912, 256], P('height')
All inputs are finite; a program needn't handle non-finite values.
Results may differ from a plain program's by a relative error of at most 0.013.
Values may be sent and summed in bfloat16 or wider, within the bound.
No kernel may reach another device: no remote copies, remote signals or barrier semaphores. Data moves between devices by JAX's collectives and lax.ppermute only.
A program may use at most 128 MiB of HBM per device.

v0:
```python
import math
import jax
import jax.numpy as jnp
from jax import lax
from jax.sharding import PartitionSpec as P


def shifted(value, axis, by):
    count = lax.axis_size(axis)
    pairs = [(i, i + by) for i in range(count) if 0 <= i + by < count]
    return lax.ppermute(value, axis, pairs)


def extended_2(cells, sides, width):
    for axis, dim in sides:
        count = lax.axis_size(axis)
        ends = count - 1
        head = lax.slice_in_dim(cells, 0, width, axis=dim)
        tail = lax.slice_in_dim(cells, cells.shape[dim] - width, cells.shape[dim], axis=dim)
        cells = jnp.concatenate(
            [
                lax.ppermute(tail, axis, [(i, (i + 1) % count) for i in range(ends)]),
                cells,
                lax.ppermute(head, axis, [((i + 1) % count, i) for i in range(ends)]),
            ],
            axis=dim,
        )
    return cells


def tap_offsets():
    return [(t_off, h_off, w_off) for t_off in range(3) for h_off in range(3) for w_off in range(3)]


def widen(stacked):
    return jnp.pad(stacked, ((0, 0), (0, 0), (1, 1), (0, 0)))


def clip_edges(rimmed):
    place = lax.axis_index("height")
    blocks = lax.axis_size("height")
    rows_n = rimmed.shape[1]
    row_ids = jnp.arange(rows_n, dtype=jnp.int32)
    cut = jnp.logical_or(
        jnp.logical_and(row_ids == 0, place == 0),
        jnp.logical_and(row_ids == rows_n - 1, place == blocks - 1),
    )
    return jnp.where(cut[None, :, None, None], jnp.zeros_like(rimmed), rimmed)


def causal_patches(values):
    frames_n, height_n, width_n, chans = values.shape
    earlier = shifted(values, "tm", 1)
    extended = jnp.concatenate([earlier, values], axis=0)
    rimmed = clip_edges(extended_2(extended, (("height", 1),), 1))
    padded = widen(rimmed)
    pieces = [
        padded[t_off : t_off + frames_n, h_off : h_off + height_n, w_off : w_off + width_n]
        for t_off, h_off, w_off in tap_offsets()
    ]
    return jnp.stack(pieces, axis=3).reshape(frames_n * height_n * width_n, 27 * chans)


def future_patches(grads):
    frames_n, height_n, width_n, chans = grads.shape
    later = shifted(grads, "tm", -1)
    extended = jnp.concatenate([grads, later], axis=0)
    rimmed = clip_edges(extended_2(extended, (("height", 1),), 1))
    padded = widen(rimmed)
    pieces = [
        padded[
            2 - t_off : 2 - t_off + frames_n,
            2 - h_off : 2 - h_off + height_n,
            2 - w_off : 2 - w_off + width_n,
        ]
        for t_off, h_off, w_off in tap_offsets()
    ]
    return jnp.stack(pieces, axis=3).reshape(frames_n * height_n * width_n, 27, chans)


def reduce_grad(local_grad):
    owned = lax.psum_scatter(
        local_grad.astype(jnp.bfloat16), "height", scatter_dimension=0, tiled=True
    )
    return lax.psum(owned, "tm").astype(jnp.float32)


def shards(clip, teacher, kernel_one, kernel_two):
    frames_n, height_n, width_n, chans = clip.shape
    full_one = lax.all_gather(kernel_one, "height", axis=0, tiled=True)
    patches_clip = causal_patches(clip)
    pre_act = jnp.dot(patches_clip, full_one, preferred_element_type=jnp.float32)
    hidden = jax.nn.silu(pre_act).astype(jnp.bfloat16)
    full_two = lax.all_gather(kernel_two, "height", axis=0, tiled=True)
    patches_hidden = causal_patches(hidden.reshape(frames_n, height_n, width_n, chans))
    branch = jnp.dot(patches_hidden, full_two, preferred_element_type=jnp.float32)
    output = clip.reshape(-1, chans).astype(jnp.float32) + branch
    count_all = frames_n * lax.axis_size("tm") * height_n * lax.axis_size("height") * width_n
    factor = 1.0 / math.sqrt(count_all)
    grad_out = ((output - teacher.reshape(-1, chans).astype(jnp.float32)) * factor).astype(
        jnp.bfloat16
    )
    contract_rows = (((0,), (0,)), ((), ()))
    grad_two = reduce_grad(
        lax.dot_general(patches_hidden, grad_out, contract_rows, preferred_element_type=jnp.float32)
    )
    grad_patches = future_patches(grad_out.reshape(frames_n, height_n, width_n, chans))
    grad_hidden = jnp.einsum(
        "rkc,kdc->rd",
        grad_patches,
        full_two.reshape(27, chans, chans),
        preferred_element_type=jnp.float32,
    )
    sigmoid_pre = jax.nn.sigmoid(pre_act)
    grad_pre = (grad_hidden * sigmoid_pre * (1.0 + pre_act * (1.0 - sigmoid_pre))).astype(
        jnp.bfloat16
    )
    grad_one = reduce_grad(
        lax.dot_general(patches_clip, grad_pre, contract_rows, preferred_element_type=jnp.float32)
    )
    student = output.astype(jnp.bfloat16).reshape(frames_n, height_n, width_n, chans)
    return (student, grad_one, grad_two)


def solution(mesh):
    in_specs = (
        P("tm", "height", None, None),
        P("tm", "height", None, None),
        P("height", None),
        P("height", None),
    )
    out_specs = (P("tm", "height", None, None), P("height", None), P("height", None))
    return jax.shard_map(shards, mesh=mesh, in_specs=in_specs, out_specs=out_specs, check_vma=False)
```

profile of v0, /device:TPU:0, one launch (start us, length us, event | category | flops | bytes accessed | tf_op | source)
XLA Modules:
  0.0 475.6 jit_solution(719828073563204116)
XLA Ops:
  7.9 2.4 collective-permute-start
  13.0 4.2 collective-permute-start.1
  19.8 4.1 collective-permute-done.2
  26.5 23.9 %copy.7 = bf16[2,8,48,27,256]{4,3,2,1,0:T(8,128)(2,1)S(1)} copy(bf16[2,8,48,27,256]{4,2,1,0,3:T(8,128)(2,1)S(1)} %bitcast_dynamic-update-slice_fusion.18) | data formatting | bytes 21233664 | tf_op jit(solution)/shard_map/stack | solution.py:61
  50.4 10.2 %copy.9 = bf16[96,8,27,256]{3,1,2,0:T(8,128)(2,1)} copy(bf16[96,8,27,256]{3,2,1,0:T(8,128)(2,1)S(1)} %bitcast.205) | data formatting | bytes 21233664
  60.6 23.9 %all-gather.3.cloned.1.call-done = bf16[6912,256]{1,0:T(8,128)(2,1)} async-done(((bf16[432,256]{1,0:T(8,128)(2,1)}), bf16[6912,256]{1,0:T(8,128)(2,1)}) %all-gather.3.cloned.1.call-update) | async-done | bytes 3538960 | tf_op jit(solution)/shard_map/all_gather | solution.py:90
  84.5 8.8 %multiply_convert_fusion = (bf16[768,256]{1,0:T(8,128)(2,1)S(1)}, f32[768,256]{1,0:T(8,128)}) fusion(bf16[768,6912]{1,0:T(8,128)(2,1)} %bitcast.207, bf16[6912,256]{1,0:T(8,128)(2,1)} %all-gather.3.cloned.1.call-done), kind=kOutput, calls=%fused_computation.16 | convolution fusion | flops 2718892032 | bytes 15335424 | tf_op jit(solution)/shard_map/dot_general | solution.py:92
  95.9 3.4 collective-permute-start.4
  101.8 4.1 collective-permute-done.5
  108.6 23.9 %copy.8 = bf16[2,8,48,27,256]{4,3,2,1,0:T(8,128)(2,1)S(1)} copy(bf16[2,8,48,27,256]{4,2,1,0,3:T(8,128)(2,1)S(1)} %bitcast_dynamic-update-slice_fusion) | data formatting | bytes 21233664 | tf_op jit(solution)/shard_map/stack | solution.py:61
  132.5 10.2 %copy.10 = bf16[96,8,27,256]{3,1,2,0:T(8,128)(2,1)} copy(bf16[96,8,27,256]{3,2,1,0:T(8,128)(2,1)S(1)} %bitcast.206) | data formatting | bytes 21233664
  142.7 14.7 %all-gather.5.cloned.1.call-done = bf16[6912,256]{1,0:T(8,128)(2,1)} async-done(((bf16[432,256]{1,0:T(8,128)(2,1)}), bf16[6912,256]{1,0:T(8,128)(2,1)}) %all-gather.5.cloned.1.call-update) | async-done | bytes 3538960 | tf_op jit(solution)/shard_map/all_gather | solution.py:94
  157.4 8.8 %fusion.4 = (bf16[768,256]{1,0:T(8,128)(2,1)S(1)}, bf16[768,256]{1,0:T(8,128)(2,1)}) fusion(bf16[2,8,48,256]{3,2,1,0:T(8,128)(2,1)S(1)} %copy-done.2, bf16[768,6912]{1,0:T(8,128)(2,1)} %bitcast.209, bf16[6912,256]{1,0:T(8,128)(2,1)} %all-gather.5.cloned.1.call-done, bf16[768,256]{1,0:T(8,128)(2,1)S(1)} %bitcast.246), kind=kOutput, calls=%fused_computation.12 | convolution fusion | flops 2719285248 | bytes 15728640 | tf_op jit(solution)/shard_map/dot_general | solution.py:96
  167.6 4.5 convolution_convert_fusion
  172.2 3.4 collective-permute-start.7
  175.5 1.5 collective-permute-start.8
  178.5 6.1 %collective-permute-done.8 = bf16[4,1,48,256]{3,2,1,0:T(8,128)(2,1)S(1)} collective-permute-done((bf16[4,1,48,256]{3,2,1,0:T(8,128)(2,1)S(1)}, bf16[4,1,48,256]{3,2,1,0:T(8,128)(2,1)S(1)}, u32[]{:S(2)}, u32[]{:S(2)}) %collective-permute-start.8) | collective-permute-done | bytes 98336 | tf_op jit(solution)/shard_map/ppermute | solution.py:24
  186.6 4.0 pad_slice_fusion
  210.2 20.4 %convolution_convert_fusion.1 = bf16[6912,256]{1,0:T(8,128)(2,1)} fusion(bf16[768,6912]{1,0:T(8,128)(2,1)} %bitcast.208, bf16[768,27,256]{2,0,1:T(8,128)(2,1)} %constant_dynamic-update-slice_fusion.2, bf16[27,256,256]{2,1,0:T(8,128)(2,1)S(1)} %bitcast.247, f32[768,256]{1,0:T(8,128)} %get-tuple-element.41), kind=kOutput, calls=%fused_computation.1 | convolution fusion | flops 5439356928 | bytes 29097984 | tf_op jit(solution)/shard_map/dot_general | solution.py:119
  230.6 75.9 %reduce-scatter.5.cloned.1.call-done = bf16[432,256]{1,0:T(8,128)(2,1)} async-done(((bf16[6912,256]{1,0:T(8,128)(2,1)}), bf16[432,256]{1,0:T(8,128)(2,1)}) %reduce-scatter.5.cloned.1.call-update) | async-done | bytes 221200 | tf_op jit(solution)/shard_map/reduce_scatter | solution.py:82
  306.6 139.2 %reduce-scatter.3.cloned.1.call-done = bf16[432,256]{1,0:T(8,128)(2,1)} async-done(((bf16[6912,256]{1,0:T(8,128)(2,1)}), bf16[432,256]{1,0:T(8,128)(2,1)}) %reduce-scatter.3.cloned.1.call-update) | async-done | bytes 221200 | tf_op jit(solution)/shard_map/reduce_scatter | solution.py:82
  445.8 19.8 %all-reduce.6.cloned.1.call-done = (bf16[432,256]{1,0:T(8,128)(2,1)}, bf16[432,256]{1,0:T(8,128)(2,1)}) async-done(((bf16[432,256]{1,0:T(8,128)(2,1)}, bf16[432,256]{1,0:T(8,128)(2,1)}), (bf16[432,256]{1,0:T(8,128)(2,1)}, bf16[432,256]{1,0:T(8,128)(2,1)})) %all-reduce.6.cloned.1.call-update) | async-done | bytes 442384 | tf_op jit(solution)/shard_map/psum | solution.py:85
  465.6 1.7 convert_element_type.49
  467.3 1.7 convert_element_type.51
  (124 shorter events, 40.5 us)
Async XLA Ops:
  7.2 77.3 %all-gather.3.cloned.1.call-start = ((), (), s32[]{:S(2)}) async-start(), calls=%async_computation.2 | async-start | bytes 3760128 | tf_op jit(solution)/shard_map/all_gather | solution.py:90
  7.9 149.5 %all-gather.5.cloned.1.call-start = ((), (), s32[]{:S(2)}) async-start(), calls=%async_computation.3 | async-start | bytes 3760128 | tf_op jit(solution)/shard_map/all_gather | solution.py:94
  7.9 3.9 collective-permute-start
  10.4 296.2 %reduce-scatter.5.cloned.1.call-start = ((), (), s32[]{:S(2)}) async-start(), calls=%async_computation.5 | async-start | bytes 3760128 | tf_op jit(solution)/shard_map/reduce_scatter | solution.py:82
  13.0 6.8 %collective-permute-start.1 = (bf16[4,1,48,256]{3,2,1,0:T(8,128)(2,1)S(1)}, bf16[4,1,48,256]{3,2,1,0:T(8,128)(2,1)S(1)}, u32[]{:S(2)}, u32[]{:S(2)}) collective-permute-start(bf16[4,1,48,256]{3,2,1,0:T(8,128)(2,1)S(1)} %get-tuple-element.38), channel_id=1, source_target_pairs={{0,1},{1,2},{2,3},{3,4},{4,5},{5,6},{6,7},{7,8},{8,9},{9,10},{10,1... | collective-permute-start | bytes 294920 | tf_op jit(solution)/shard_map/ppermute | solution.py:22
  17.2 6.7 %collective-permute-start.2 = (bf16[4,1,48,256]{3,2,1,0:T(8,128)(2,1)S(1)}, bf16[4,1,48,256]{3,2,1,0:T(8,128)(2,1)S(1)}, u32[]{:S(2)}, u32[]{:S(2)}) collective-permute-start(bf16[4,1,48,256]{3,2,1,0:T(8,128)(2,1)S(1)} %get-tuple-element.39), channel_id=1, source_target_pairs={{1,0},{2,1},{3,2},{4,3},{5,4},{6,5},{7,6},{8,7},{9,8},{10,9},{11,1... | collective-permute-start | bytes 294920 | tf_op jit(solution)/shard_map/ppermute | solution.py:24
  93.3 2.6 collective-permute-start.3
  95.9 5.9 %collective-permute-start.4 = (bf16[4,1,48,256]{3,2,1,0:T(8,128)(2,1)S(1)}, bf16[4,1,48,256]{3,2,1,0:T(8,128)(2,1)S(1)}, u32[]{:S(2)}, u32[]{:S(2)}) collective-permute-start(bf16[4,1,48,256]{3,2,1,0:T(8,128)(2,1)S(1)} %get-tuple-element.36), channel_id=1, source_target_pairs={{0,1},{1,2},{2,3},{3,4},{4,5},{5,6},{6,7},{7,8},{8,9},{9,10},{10,1... | collective-permute-start | bytes 294920 | tf_op jit(solution)/shard_map/ppermute | solution.py:22
  99.3 6.7 %collective-permute-start.5 = (bf16[4,1,48,256]{3,2,1,0:T(8,128)(2,1)S(1)}, bf16[4,1,48,256]{3,2,1,0:T(8,128)(2,1)S(1)}, u32[]{:S(2)}, u32[]{:S(2)}) collective-permute-start(bf16[4,1,48,256]{3,2,1,0:T(8,128)(2,1)S(1)} %get-tuple-element.37), channel_id=1, source_target_pairs={{1,0},{2,1},{3,2},{4,3},{5,4},{6,5},{7,6},{8,7},{9,8},{10,9},{11,1... | collective-permute-start | bytes 294920 | tf_op jit(solution)/shard_map/ppermute | solution.py:24
  132.5 24.9 %copy-start = (bf16[2,8,48,256]{3,2,1,0:T(8,128)(2,1)S(1)}, bf16[2,8,48,256]{3,2,1,0:T(8,128)(2,1)}, u32[]{:S(2)}) copy-start(bf16[2,8,48,256]{3,2,1,0:T(8,128)(2,1)} %param.4) | copy-start | bytes 1179652
  132.5 24.9 %copy-start.2 = (bf16[2,8,48,256]{3,2,1,0:T(8,128)(2,1)S(1)}, bf16[2,8,48,256]{3,2,1,0:T(8,128)(2,1)}, u32[]{:S(2)}) copy-start(bf16[2,8,48,256]{3,2,1,0:T(8,128)(2,1)} %param.5) | copy-start | bytes 1179652
  142.7 24.8 %slice-start = ((s8[10616832]{0:T(1024)(128)(4,1)}), s8[2228224]{0:T(1024)(128)(4,1)S(1)}, s32[]{:S(2)}) async-start(s8[10616832]{0:T(1024)(128)(4,1)} %bitcast.210), calls=%async_computation.7 | async-start | bytes 4456448
  157.4 10.1 %slice-start.1 = ((s8[10616832]{0:T(1024)(128)(4,1)}), s8[4194304]{0:T(1024)(128)(4,1)S(1)}, s32[]{:S(2)}) async-start(s8[10616832]{0:T(1024)(128)(4,1)} %bitcast.210), calls=%async_computation.8 | async-start | bytes 8388608
  157.4 10.1 %slice-start.2 = ((s8[10616832]{0:T(1024)(128)(4,1)}), s8[4194304]{0:T(1024)(128)(4,1)S(1)}, s32[]{:S(2)}) async-start(s8[10616832]{0:T(1024)(128)(4,1)} %bitcast.210), calls=%async_computation.9 | async-start | bytes 8388608
  166.2 5.9 %collective-permute-start.6 = (bf16[2,8,48,256]{3,2,1,0:T(8,128)(2,1)S(1)}, bf16[2,8,48,256]{3,2,1,0:T(8,128)(2,1)S(1)}, u32[]{:S(2)}, u32[]{:S(2)}) collective-permute-start(bf16[2,8,48,256]{3,2,1,0:T(8,128)(2,1)S(1)} %bitcast.232), channel_id=1, source_target_pairs={{16,0},{17,1},{18,2},{19,3},{20,4},{21,5},{22,6},{23,7},{24,8},{25... | collective-permute-start | bytes 1179656 | tf_op jit(solution)/shard_map/ppermute | solution.py:11
  172.1 273.7 %reduce-scatter.3.cloned.1.call-start = ((), (), s32[]{:S(2)}) async-start(), calls=%async_computation.4 | async-start | bytes 3760128 | tf_op jit(solution)/shard_map/reduce_scatter | solution.py:82
  172.2 6.3 %collective-permute-start.7 = (bf16[4,1,48,256]{3,2,1,0:T(8,128)(2,1)S(1)}, bf16[4,1,48,256]{3,2,1,0:T(8,128)(2,1)S(1)}, u32[]{:S(2)}, u32[]{:S(2)}) collective-permute-start(bf16[4,1,48,256]{3,2,1,0:T(8,128)(2,1)S(1)} %get-tuple-element.32), channel_id=1, source_target_pairs={{0,1},{1,2},{2,3},{3,4},{4,5},{5,6},{6,7},{7,8},{8,9},{9,10},{10,1... | collective-permute-start | bytes 294920 | tf_op jit(solution)/shard_map/ppermute | solution.py:22
  175.5 9.0 %collective-permute-start.8 = (bf16[4,1,48,256]{3,2,1,0:T(8,128)(2,1)S(1)}, bf16[4,1,48,256]{3,2,1,0:T(8,128)(2,1)S(1)}, u32[]{:S(2)}, u32[]{:S(2)}) collective-permute-start(bf16[4,1,48,256]{3,2,1,0:T(8,128)(2,1)S(1)} %get-tuple-element.33), channel_id=1, source_target_pairs={{1,0},{2,1},{3,2},{4,3},{5,4},{6,5},{7,6},{8,7},{9,8},{10,9},{11,1... | collective-permute-start | bytes 294920 | tf_op jit(solution)/shard_map/ppermute | solution.py:24
  190.6 19.6 %copy-start.1 = (bf16[6912,256]{1,0:T(8,128)(2,1)S(1)}, bf16[6912,256]{1,0:T(8,128)(2,1)}, u32[]{:S(2)}) copy-start(bf16[6912,256]{1,0:T(8,128)(2,1)} %all-gather.5.cloned.1.call-done) | copy-start | bytes 10616836
  230.6 235.0 %all-reduce.6.cloned.1.call-start = ((), (), s32[]{:S(2)}) async-start(), calls=%async_computation.6 | async-start | bytes 884736 | tf_op jit(solution)/shard_map/psum | solution.py:85
Sparse Core Ops, SparseCore 0:
  10.8 73.6 all-gather.2
  87.3 70.1 all-gather.4
  172.2 134.3 reduce-scatter.4
  311.5 134.1 reduce-scatter.2
  448.0 17.5 all-reduce.5
where the time goes:
time: 476 us
  waiting for transfers between devices  295 us (62%)
  local copies, waits for them, and re-layouts  99.1 us (21%)
  matrix products  42.5 us (9%)
  starting transfers between devices  20.4 us (4%)
  between operations  14.3 us (3%)
    reduce_scatter x2, waiting for transfers between devices, reduce_grad(): lax.psum_scatter(local_grad.astype(jnp.bfloat16), 'height', scatter_dimen...  215 us
    another operation x4, local copies, waits for them, and re-layouts, causal_patches(): jnp.stack(pieces, axis=3).reshape(frames_n * height_n * width_n, 27 * chans)  47.9 us
    unnamed x93, local copies, waits for them, and re-layouts  45.1 us
    all_gather x1, waiting for transfers between devices, shards(): full_one = lax.all_gather(kernel_one, 'height', axis=0, tiled=True)  23.9 us
    dot_general x1, matrix products, shards(): lax.dot_general(patches_clip, grad_pre, contract_rows, preferred_element_...  20.4 us
    psum x1, waiting for transfers between devices, reduce_grad(): return lax.psum(owned, 'tm').astype(jnp.float32)  19.8 us
    all_gather x1, waiting for transfers between devices, shards(): full_two = lax.all_gather(kernel_two, 'height', axis=0, tiled=True)  14.7 us
    ppermute x3, waiting for transfers between devices, extended_2(): lax.ppermute(head, axis, [((i + 1) % count, i) for i in range(ends)])  14.3 us
  transfers between devices with their start and end apart: 14, of which 13 were waited for; matrix products, arithmetic and copies ran while one was open for 28% of the time, Pallas kernels for 0%

commit v1 on v0

--- a/solution.py
+++ b/solution.py
@@ -3,6 +3,12 @@
 import jax.numpy as jnp
 from jax import lax
 from jax.sharding import PartitionSpec as P
+
+
+def in_order(tiles, dim):
+    tiles = jnp.moveaxis(tiles, 0, dim)
+    lengths = tiles.shape
+    return tiles.reshape(*lengths[:dim], lengths[dim] * lengths[dim + 1], *lengths[dim + 2 :])
 
 
 def shifted(value, axis, by):
@@ -87,7 +93,19 @@
 
 def shards(clip, teacher, kernel_one, kernel_two):
     frames_n, height_n, width_n, chans = clip.shape
-    full_one = lax.all_gather(kernel_one, "height", axis=0, tiled=True)
+    count_2 = lax.axis_size("height")
+    pairs_2 = [(i_2, (i_2 + 1) % count_2) for i_2 in range(count_2)]
+    back = [(b, a) for a, b in pairs_2]
+    lower, upper = ([], [])
+    for step in range(count_2 - 1):
+        if step % 2 == 0:
+            lower.append(lax.ppermute(lower[-1] if lower else kernel_one, "height", pairs_2))
+        else:
+            upper.append(lax.ppermute(upper[-1] if upper else kernel_one, "height", back))
+    blocks_2 = jnp.stack([*lower[::-1], kernel_one, *upper])
+    shift = lax.axis_index("height") - len(lower)
+    blocks_2 = blocks_2[(jnp.arange(count_2) - shift) % count_2]
+    full_one = in_order(blocks_2, 0)
     patches_clip = causal_patches(clip)
     pre_act = jnp.dot(patches_clip, full_one, preferred_element_type=jnp.float32)
     hidden = jax.nn.silu(pre_act).astype(jnp.bfloat16)

time: 476 us -> 528 us (1.11)
  starting transfers between devices: 20.4 us -> 60.8 us
  waiting for transfers between devices: 295 us -> 303 us
    ppermute x0 -> x15, waiting for transfers between devices: none -> 52.5 us  [the longest x8 44.2 us: shards(): lax.ppermute(lower[-1] if lower else kernel_one, 'height', pairs_2)]
    ppermute x0 -> x15, starting transfers between devices: none -> 42.1 us  [the longest x7 30.8 us: shards(): lax.ppermute(upper[-1] if upper else kernel_one, 'height', back)]
    all_gather x1 -> x0, waiting for transfers between devices: 23.9 us -> none  [shards(): full_one = lax.all_gather(kernel_one, 'height', axis=0, tiled=True)]
    all_gather x1, waiting for transfers between devices: 14.7 us -> 0.01 us  [shards(): full_two = lax.all_gather(kernel_two, 'height', axis=0, tiled=True)]
    ppermute x3, waiting for transfers between devices: 14.3 us -> 8.75 us  [extended_2(): lax.ppermute(head, axis, [((i + 1) % count, i) for i in range(ends)])]
    unnamed x93 -> x118, local copies, waits for them, and re-layouts: 45.1 us -> 45.5 us
  transfers between devices with their start and end apart: 14 -> 28, of which waited for: 13 -> 20; matrix products, arithmetic and copies ran while one was open for 28% -> 26% of each run, Pallas kernels for 0% -> 0%
where the time goes in v1:
time: 528 us; the launch traced here: 527 us
  waiting for transfers between devices  303 us (57%)
  local copies, waits for them, and re-layouts  102 us (19%)
  starting transfers between devices  60.8 us (12%)
  matrix products  42.4 us (8%)
  between operations  14.6 us (3%)
    reduce_scatter x2, waiting for transfers between devices, reduce_grad(): lax.psum_scatter(local_grad.astype(jnp.bfloat16), 'height', scatter_dimen...  218 us
    another operation x4, local copies, waits for them, and re-layouts, causal_patches(): jnp.stack(pieces, axis=3).reshape(frames_n * height_n * width_n, 27 * chans)  47.9 us
    unnamed x118, local copies, waits for them, and re-layouts  45.5 us
    ppermute x8, waiting for transfers between devices, shards(): lax.ppermute(lower[-1] if lower else kernel_one, 'height', pairs_2)  44.2 us
    ppermute x7, starting transfers between devices, shards(): lax.ppermute(upper[-1] if upper else kernel_one, 'height', back)  30.8 us
    dot_general x1, matrix products, shards(): lax.dot_general(patches_clip, grad_pre, contract_rows, preferred_element_...  20.3 us
    psum x1, waiting for transfers between devices, reduce_grad(): return lax.psum(owned, 'tm').astype(jnp.float32)  19.8 us
    ppermute x8, starting transfers between devices, shards(): lax.ppermute(lower[-1] if lower else kernel_one, 'height', pairs_2)  11.3 us
  transfers between devices with their start and end apart: 28, of which 20 were waited for; matrix products, arithmetic and copies ran while one was open for 26% of the time, Pallas kernels for 0%

profile of v1, /device:TPU:0, one launch (start us, length us, event | category | flops | bytes accessed | tf_op | source)
XLA Modules:
  0.0 527.2 jit_solution(3432322773522989440)
XLA Ops:
  16.2 5.9 %collective-permute-done.3 = bf16[432,256]{1,0:T(8,128)(2,1)S(1)} collective-permute-done((bf16[432,256]{1,0:T(8,128)(2,1)}, bf16[432,256]{1,0:T(8,128)(2,1)S(1)}, u32[]{:S(2)}, u32[]{:S(2)}) %collective-permute-start.3) | collective-permute-done | bytes 221216 | tf_op jit(solution)/shard_map/ppermute | solution.py:102
  24.7 4.9 collective-permute-start.12
  36.7 6.1 %collective-permute-start.13 = (bf16[432,256]{1,0:T(8,128)(2,1)S(1)}, bf16[432,256]{1,0:T(8,128)(2,1)S(1)}, u32[]{:S(2)}, u32[]{:S(2)}) collective-permute-start(bf16[432,256]{1,0:T(8,128)(2,1)S(1)} %collective-permute-done.12), channel_id=1, source_target_pairs={{1,0},{2,1},{3,2},{4,3},{5,4},{6,5},{7,6},{8,7},{9,8},{10,9},{11,1... | collective-permute-start | bytes 663560 | tf_op jit(solution)/shard_map/ppermute | solution.py:104
  44.7 4.6 collective-permute-done.5
  51.8 8.4 %collective-permute-done.6 = bf16[432,256]{1,0:T(8,128)(2,1)S(1)} collective-permute-done((bf16[432,256]{1,0:T(8,128)(2,1)S(1)}, bf16[432,256]{1,0:T(8,128)(2,1)S(1)}, u32[]{:S(2)}, u32[]{:S(2)}) %collective-permute-start.6) | collective-permute-done | bytes 221216 | tf_op jit(solution)/shard_map/ppermute | solution.py:102
  60.5 5.7 %collective-permute-start.14 = (bf16[432,256]{1,0:T(8,128)(2,1)S(1)}, bf16[432,256]{1,0:T(8,128)(2,1)S(1)}, u32[]{:S(2)}, u32[]{:S(2)}) collective-permute-start(bf16[432,256]{1,0:T(8,128)(2,1)S(1)} %collective-permute-done.13), channel_id=1, source_target_pairs={{1,0},{2,1},{3,2},{4,3},{5,4},{6,5},{7,6},{8,7},{9,8},{10,9},{11,1... | collective-permute-start | bytes 663560 | tf_op jit(solution)/shard_map/ppermute | solution.py:104
  66.2 5.5 %collective-permute-done.7 = bf16[432,256]{1,0:T(8,128)(2,1)S(1)} collective-permute-done((bf16[432,256]{1,0:T(8,128)(2,1)S(1)}, bf16[432,256]{1,0:T(8,128)(2,1)S(1)}, u32[]{:S(2)}, u32[]{:S(2)}) %collective-permute-start.7) | collective-permute-done | bytes 221216 | tf_op jit(solution)/shard_map/ppermute | solution.py:102
  72.9 4.5 collective-permute-start.15
  77.4 10.0 %collective-permute-done.8 = bf16[432,256]{1,0:T(8,128)(2,1)S(1)} collective-permute-done((bf16[432,256]{1,0:T(8,128)(2,1)S(1)}, bf16[432,256]{1,0:T(8,128)(2,1)S(1)}, u32[]{:S(2)}, u32[]{:S(2)}) %collective-permute-start.8) | collective-permute-done | bytes 221216 | tf_op jit(solution)/shard_map/ppermute | solution.py:102
  93.3 8.7 %collective-permute-done.9 = bf16[432,256]{1,0:T(8,128)(2,1)S(1)} collective-permute-done((bf16[432,256]{1,0:T(8,128)(2,1)S(1)}, bf16[432,256]{1,0:T(8,128)(2,1)S(1)}, u32[]{:S(2)}, u32[]{:S(2)}) %collective-permute-start.9) | collective-permute-done | bytes 221216 | tf_op jit(solution)/shard_map/ppermute | solution.py:102
  104.5 23.9 %copy.7 = bf16[2,8,48,27,256]{4,3,2,1,0:T(8,128)(2,1)S(1)} copy(bf16[2,8,48,27,256]{4,2,1,0,3:T(8,128)(2,1)S(1)} %bitcast_dynamic-update-slice_fusion.18) | data formatting | bytes 21233664 | tf_op jit(solution)/shard_map/stack | solution.py:67
  128.4 10.2 %copy.9 = bf16[96,8,27,256]{3,1,2,0:T(8,128)(2,1)} copy(bf16[96,8,27,256]{3,2,1,0:T(8,128)(2,1)S(1)} %bitcast.240) | data formatting | bytes 21233664
  147.9 8.8 %multiply_convert_fusion = (bf16[768,256]{1,0:T(8,128)(2,1)S(1)}, f32[768,256]{1,0:T(8,128)}) fusion(bf16[768,6912]{1,0:T(8,128)(2,1)} %bitcast.242, bf16[6912,256]{1,0:T(8,128)(2,1)} %bitcast.248), kind=kOutput, calls=%fused_computation.17 | convolution fusion | flops 2718892032 | bytes 15335424 | tf_op jit(solution)/shard_map/dot_general | solution.py:110
  164.1 4.1 collective-permute-done.20
  170.9 23.9 %copy.8 = bf16[2,8,48,27,256]{4,3,2,1,0:T(8,128)(2,1)S(1)} copy(bf16[2,8,48,27,256]{4,2,1,0,3:T(8,128)(2,1)S(1)} %bitcast_dynamic-update-slice_fusion) | data formatting | bytes 21233664 | tf_op jit(solution)/shard_map/stack | solution.py:67
  194.8 10.2 %copy.10 = bf16[96,8,27,256]{3,1,2,0:T(8,128)(2,1)} copy(bf16[96,8,27,256]{3,2,1,0:T(8,128)(2,1)S(1)} %bitcast.241) | data formatting | bytes 21233664
  205.1 8.8 %fusion.4 = (bf16[768,256]{1,0:T(8,128)(2,1)S(1)}, bf16[768,256]{1,0:T(8,128)(2,1)}) fusion(bf16[2,8,48,256]{3,2,1,0:T(8,128)(2,1)S(1)} %copy-done.7, bf16[768,6912]{1,0:T(8,128)(2,1)} %bitcast.244, bf16[6912,256]{1,0:T(8,128)(2,1)} %all-gather.2.cloned.1.call-done, bf16[768,256]{1,0:T(8,128)(2,1)S(1)} %bitcast.282), kind=kOutput, calls=%fused_computation.13 | convolution fusion | flops 2719285248 | bytes 15728640 | tf_op jit(solution)/shard_map/dot_general | solution.py:114
  215.2 4.5 convolution_convert_fusion
  219.8 5.7 %collective-permute-start.22 = (bf16[4,1,48,256]{3,2,1,0:T(8,128)(2,1)S(1)}, bf16[4,1,48,256]{3,2,1,0:T(8,128)(2,1)S(1)}, u32[]{:S(2)}, u32[]{:S(2)}) collective-permute-start(bf16[4,1,48,256]{3,2,1,0:T(8,128)(2,1)S(1)} %get-tuple-element.32), channel_id=1, source_target_pairs={{0,1},{1,2},{2,3},{3,4},{4,5},{5,6},{6,7},{7,8},{8,9},{9,10},{10,1... | collective-permute-start | bytes 294920 | tf_op jit(solution)/shard_map/ppermute | solution.py:28
  228.5 4.6 collective-permute-done.23
  258.8 20.3 %convolution_convert_fusion.1 = bf16[6912,256]{1,0:T(8,128)(2,1)} fusion(bf16[768,6912]{1,0:T(8,128)(2,1)} %bitcast.243, bf16[768,27,256]{2,0,1:T(8,128)(2,1)} %constant_dynamic-update-slice_fusion.2, bf16[27,256,256]{2,1,0:T(8,128)(2,1)S(1)} %bitcast.283, f32[768,256]{1,0:T(8,128)} %get-tuple-element.41), kind=kOutput, calls=%fused_computation.2 | convolution fusion | flops 5439356928 | bytes 29097984 | tf_op jit(solution)/shard_map/dot_general | solution.py:137
  279.2 78.9 %reduce-scatter.5.cloned.1.call-done = bf16[432,256]{1,0:T(8,128)(2,1)} async-done(((bf16[6912,256]{1,0:T(8,128)(2,1)}), bf16[432,256]{1,0:T(8,128)(2,1)}) %reduce-scatter.5.cloned.1.call-update) | async-done | bytes 221200 | tf_op jit(solution)/shard_map/reduce_scatter | solution.py:88
  358.1 139.4 %reduce-scatter.3.cloned.1.call-done = bf16[432,256]{1,0:T(8,128)(2,1)} async-done(((bf16[6912,256]{1,0:T(8,128)(2,1)}), bf16[432,256]{1,0:T(8,128)(2,1)}) %reduce-scatter.3.cloned.1.call-update) | async-done | bytes 221200 | tf_op jit(solution)/shard_map/reduce_scatter | solution.py:88
  497.5 19.8 %all-reduce.6.cloned.1.call-done = (bf16[432,256]{1,0:T(8,128)(2,1)}, bf16[432,256]{1,0:T(8,128)(2,1)}) async-done(((bf16[432,256]{1,0:T(8,128)(2,1)}, bf16[432,256]{1,0:T(8,128)(2,1)}), (bf16[432,256]{1,0:T(8,128)(2,1)}, bf16[432,256]{1,0:T(8,128)(2,1)})) %all-reduce.6.cloned.1.call-update) | async-done | bytes 442384 | tf_op jit(solution)/shard_map/psum | solution.py:91
  (180 shorter events, 85.4 us)
Async XLA Ops:
  7.2 197.9 %all-gather.2.cloned.1.call-start = ((), (), s32[]{:S(2)}) async-start(), calls=%async_computation.2 | async-start | bytes 3760128 | tf_op jit(solution)/shard_map/all_gather | solution.py:112
  7.2 22.4 %collective-permute-start = (bf16[2,8,48,256]{3,2,1,0:T(8,128)(2,1)}, bf16[2,8,48,256]{3,2,1,0:T(8,128)(2,1)S(1)}, u32[]{:S(2)}, u32[]{:S(2)}) collective-permute-start(bf16[2,8,48,256]{3,2,1,0:T(8,128)(2,1)} %param.4), channel_id=1, source_target_pairs={{0,16},{1,17},{2,18},{3,19},{4,20},{5,21},{6,22},{7,23},{8,24},{9,... | collective-permute-start | bytes 1179656 | tf_op jit(solution)/shard_map/ppermute | solution.py:17
  9.6 12.5 %collective-permute-start.3 = (bf16[432,256]{1,0:T(8,128)(2,1)}, bf16[432,256]{1,0:T(8,128)(2,1)S(1)}, u32[]{:S(2)}, u32[]{:S(2)}) collective-permute-start(bf16[432,256]{1,0:T(8,128)(2,1)} %param.6), channel_id=1, source_target_pairs={{0,1},{1,2},{2,3},{3,4},{4,5},{5,6},{6,7},{7,8},{8,9},{9,10},{10,1... | collective-permute-start | bytes 663560 | tf_op jit(solution)/shard_map/ppermute | solution.py:102
  12.0 12.7 %collective-permute-start.11 = (bf16[432,256]{1,0:T(8,128)(2,1)}, bf16[432,256]{1,0:T(8,128)(2,1)S(1)}, u32[]{:S(2)}, u32[]{:S(2)}) collective-permute-start(bf16[432,256]{1,0:T(8,128)(2,1)} %param.6), channel_id=1, source_target_pairs={{1,0},{2,1},{3,2},{4,3},{5,4},{6,5},{7,6},{8,7},{9,8},{10,9},{11,1... | collective-permute-start | bytes 663560 | tf_op jit(solution)/shard_map/ppermute | solution.py:104
  16.1 342.0 %reduce-scatter.5.cloned.1.call-start = ((), (), s32[]{:S(2)}) async-start(), calls=%async_computation.4 | async-start | bytes 3760128 | tf_op jit(solution)/shard_map/reduce_scatter | solution.py:88
  22.1 12.4 %collective-permute-start.4 = (bf16[432,256]{1,0:T(8,128)(2,1)S(1)}, bf16[432,256]{1,0:T(8,128)(2,1)S(1)}, u32[]{:S(2)}, u32[]{:S(2)}) collective-permute-start(bf16[432,256]{1,0:T(8,128)(2,1)S(1)} %collective-permute-done.3), channel_id=1, source_target_pairs={{0,1},{1,2},{2,3},{3,4},{4,5},{5,6},{6,7},{7,8},{8,9},{9,10},{10,1... | collective-permute-start | bytes 663560 | tf_op jit(solution)/shard_map/ppermute | solution.py:102
  24.7 11.9 %collective-permute-start.12 = (bf16[432,256]{1,0:T(8,128)(2,1)S(1)}, bf16[432,256]{1,0:T(8,128)(2,1)S(1)}, u32[]{:S(2)}, u32[]{:S(2)}) collective-permute-start(bf16[432,256]{1,0:T(8,128)(2,1)S(1)} %collective-permute-done.11), channel_id=1, source_target_pairs={{1,0},{2,1},{3,2},{4,3},{5,4},{6,5},{7,6},{8,7},{9,8},{10,9},{11,1... | collective-permute-start | bytes 663560 | tf_op jit(solution)/shard_map/ppermute | solution.py:104
  30.7 12.0 %collective-permute-start.1 = (bf16[4,1,48,256]{3,2,1,0:T(8,128)(2,1)S(1)}, bf16[4,1,48,256]{3,2,1,0:T(8,128)(2,1)S(1)}, u32[]{:S(2)}, u32[]{:S(2)}) collective-permute-start(bf16[4,1,48,256]{3,2,1,0:T(8,128)(2,1)S(1)} %get-tuple-element.38), channel_id=1, source_target_pairs={{0,1},{1,2},{2,3},{3,4},{4,5},{5,6},{6,7},{7,8},{8,9},{9,10},{10,1... | collective-permute-start | bytes 294920 | tf_op jit(solution)/shard_map/ppermute | solution.py:28
  32.0 10.7 %collective-permute-start.2 = (bf16[4,1,48,256]{3,2,1,0:T(8,128)(2,1)S(1)}, bf16[4,1,48,256]{3,2,1,0:T(8,128)(2,1)S(1)}, u32[]{:S(2)}, u32[]{:S(2)}) collective-permute-start(bf16[4,1,48,256]{3,2,1,0:T(8,128)(2,1)S(1)} %get-tuple-element.39), channel_id=1, source_target_pairs={{1,0},{2,1},{3,2},{4,3},{5,4},{6,5},{7,6},{8,7},{9,8},{10,9},{11,1... | collective-permute-start | bytes 294920 | tf_op jit(solution)/shard_map/ppermute | solution.py:30
  34.5 14.8 %collective-permute-start.5 = (bf16[432,256]{1,0:T(8,128)(2,1)S(1)}, bf16[432,256]{1,0:T(8,128)(2,1)S(1)}, u32[]{:S(2)}, u32[]{:S(2)}) collective-permute-start(bf16[432,256]{1,0:T(8,128)(2,1)S(1)} %collective-permute-done.4), channel_id=1, source_target_pairs={{0,1},{1,2},{2,3},{3,4},{4,5},{5,6},{6,7},{7,8},{8,9},{9,10},{10,1... | collective-permute-start | bytes 663560 | tf_op jit(solution)/shard_map/ppermute | solution.py:102
  36.7 23.8 %collective-permute-start.13 = (bf16[432,256]{1,0:T(8,128)(2,1)S(1)}, bf16[432,256]{1,0:T(8,128)(2,1)S(1)}, u32[]{:S(2)}, u32[]{:S(2)}) collective-permute-start(bf16[432,256]{1,0:T(8,128)(2,1)S(1)} %collective-permute-done.12), channel_id=1, source_target_pairs={{1,0},{2,1},{3,2},{4,3},{5,4},{6,5},{7,6},{8,7},{9,8},{10,9},{11,1... | collective-permute-start | bytes 663560 | tf_op jit(solution)/shard_map/ppermute | solution.py:104
  49.3 10.9 %collective-permute-start.6 = (bf16[432,256]{1,0:T(8,128)(2,1)S(1)}, bf16[432,256]{1,0:T(8,128)(2,1)S(1)}, u32[]{:S(2)}, u32[]{:S(2)}) collective-permute-start(bf16[432,256]{1,0:T(8,128)(2,1)S(1)} %collective-permute-done.5), channel_id=1, source_target_pairs={{0,1},{1,2},{2,3},{3,4},{4,5},{5,6},{6,7},{7,8},{8,9},{9,10},{10,1... | collective-permute-start | bytes 663560 | tf_op jit(solution)/shard_map/ppermute | solution.py:102
  60.3 11.4 %collective-permute-start.7 = (bf16[432,256]{1,0:T(8,128)(2,1)S(1)}, bf16[432,256]{1,0:T(8,128)(2,1)S(1)}, u32[]{:S(2)}, u32[]{:S(2)}) collective-permute-start(bf16[432,256]{1,0:T(8,128)(2,1)S(1)} %collective-permute-done.6), channel_id=1, source_target_pairs={{0,1},{1,2},{2,3},{3,4},{4,5},{5,6},{6,7},{7,8},{8,9},{9,10},{10,1... | collective-permute-start | bytes 663560 | tf_op jit(solution)/shard_map/ppermute | solution.py:102
  60.5 12.4 %collective-permute-start.14 = (bf16[432,256]{1,0:T(8,128)(2,1)S(1)}, bf16[432,256]{1,0:T(8,128)(2,1)S(1)}, u32[]{:S(2)}, u32[]{:S(2)}) collective-permute-start(bf16[432,256]{1,0:T(8,128)(2,1)S(1)} %collective-permute-done.13), channel_id=1, source_target_pairs={{1,0},{2,1},{3,2},{4,3},{5,4},{6,5},{7,6},{8,7},{9,8},{10,9},{11,1... | collective-permute-start | bytes 663560 | tf_op jit(solution)/shard_map/ppermute | solution.py:104
  71.7 15.7 %collective-permute-start.8 = (bf16[432,256]{1,0:T(8,128)(2,1)S(1)}, bf16[432,256]{1,0:T(8,128)(2,1)S(1)}, u32[]{:S(2)}, u32[]{:S(2)}) collective-permute-start(bf16[432,256]{1,0:T(8,128)(2,1)S(1)} %collective-permute-done.7), channel_id=1, source_target_pairs={{0,1},{1,2},{2,3},{3,4},{4,5},{5,6},{6,7},{7,8},{8,9},{9,10},{10,1... | collective-permute-start | bytes 663560 | tf_op jit(solution)/shard_map/ppermute | solution.py:102
  72.9 18.0 %collective-permute-start.15 = (bf16[432,256]{1,0:T(8,128)(2,1)S(1)}, bf16[432,256]{1,0:T(8,128)(2,1)S(1)}, u32[]{:S(2)}, u32[]{:S(2)}) collective-permute-start(bf16[432,256]{1,0:T(8,128)(2,1)S(1)} %collective-permute-done.14), channel_id=1, source_target_pairs={{1,0},{2,1},{3,2},{4,3},{5,4},{6,5},{7,6},{8,7},{9,8},{10,9},{11,1... | collective-permute-start | bytes 663560 | tf_op jit(solution)/shard_map/ppermute | solution.py:104
  87.4 14.6 %collective-permute-start.9 = (bf16[432,256]{1,0:T(8,128)(2,1)S(1)}, bf16[432,256]{1,0:T(8,128)(2,1)S(1)}, u32[]{:S(2)}, u32[]{:S(2)}) collective-permute-start(bf16[432,256]{1,0:T(8,128)(2,1)S(1)} %collective-permute-done.8), channel_id=1, source_target_pairs={{0,1},{1,2},{2,3},{3,4},{4,5},{5,6},{6,7},{7,8},{8,9},{9,10},{10,1... | collective-permute-start | bytes 663560 | tf_op jit(solution)/shard_map/ppermute | solution.py:102
  90.8 47.8 %collective-permute-start.16 = (bf16[432,256]{1,0:T(8,128)(2,1)S(1)}, bf16[432,256]{1,0:T(8,128)(2,1)S(1)}, u32[]{:S(2)}, u32[]{:S(2)}) collective-permute-start(bf16[432,256]{1,0:T(8,128)(2,1)S(1)} %collective-permute-done.15), channel_id=1, source_target_pairs={{1,0},{2,1},{3,2},{4,3},{5,4},{6,5},{7,6},{8,7},{9,8},{10,9},{11,1... | collective-permute-start | bytes 663560 | tf_op jit(solution)/shard_map/ppermute | solution.py:104
  101.9 39.9 %collective-permute-start.10 = (bf16[432,256]{1,0:T(8,128)(2,1)S(1)}, bf16[432,256]{1,0:T(8,128)(2,1)S(1)}, u32[]{:S(2)}, u32[]{:S(2)}) collective-permute-start(bf16[432,256]{1,0:T(8,128)(2,1)S(1)} %collective-permute-done.9), channel_id=1, source_target_pairs={{0,1},{1,2},{2,3},{3,4},{4,5},{5,6},{6,7},{7,8},{8,9},{9,10},{10,1... | collective-permute-start | bytes 663560 | tf_op jit(solution)/shard_map/ppermute | solution.py:102
  161.5 6.7 %collective-permute-start.20 = (bf16[4,1,48,256]{3,2,1,0:T(8,128)(2,1)S(1)}, bf16[4,1,48,256]{3,2,1,0:T(8,128)(2,1)S(1)}, u32[]{:S(2)}, u32[]{:S(2)}) collective-permute-start(bf16[4,1,48,256]{3,2,1,0:T(8,128)(2,1)S(1)} %get-tuple-element.37), channel_id=1, source_target_pairs={{1,0},{2,1},{3,2},{4,3},{5,4},{6,5},{7,6},{8,7},{9,8},{10,9},{11,1... | collective-permute-start | bytes 294920 | tf_op jit(solution)/shard_map/ppermute | solution.py:30
  219.7 277.8 %reduce-scatter.3.cloned.1.call-start = ((), (), s32[]{:S(2)}) async-start(), calls=%async_computation.3 | async-start | bytes 3760128 | tf_op jit(solution)/shard_map/reduce_scatter | solution.py:88
  219.8 8.7 %collective-permute-start.22 = (bf16[4,1,48,256]{3,2,1,0:T(8,128)(2,1)S(1)}, bf16[4,1,48,256]{3,2,1,0:T(8,128)(2,1)S(1)}, u32[]{:S(2)}, u32[]{:S(2)}) collective-permute-start(bf16[4,1,48,256]{3,2,1,0:T(8,128)(2,1)S(1)} %get-tuple-element.32), channel_id=1, source_target_pairs={{0,1},{1,2},{2,3},{3,4},{4,5},{5,6},{6,7},{7,8},{8,9},{9,10},{10,1... | collective-permute-start | bytes 294920 | tf_op jit(solution)/shard_map/ppermute | solution.py:28
  225.5 7.6 %collective-permute-start.23 = (bf16[4,1,48,256]{3,2,1,0:T(8,128)(2,1)S(1)}, bf16[4,1,48,256]{3,2,1,0:T(8,128)(2,1)S(1)}, u32[]{:S(2)}, u32[]{:S(2)}) collective-permute-start(bf16[4,1,48,256]{3,2,1,0:T(8,128)(2,1)S(1)} %get-tuple-element.33), channel_id=1, source_target_pairs={{1,0},{2,1},{3,2},{4,3},{5,4},{6,5},{7,6},{8,7},{9,8},{10,9},{11,1... | collective-permute-start | bytes 294920 | tf_op jit(solution)/shard_map/ppermute | solution.py:30
  279.1 238.1 %all-reduce.6.cloned.1.call-start = ((), (), s32[]{:S(2)}) async-start(), calls=%async_computation.5 | async-start | bytes 884736 | tf_op jit(solution)/shard_map/psum | solution.py:91
  (15 other events, 172.9 us)
Sparse Core Ops, SparseCore 0:
  16.2 92.7 all-gather.1
  219.8 138.2 reduce-scatter.4
  363.2 134.2 reduce-scatter.2
  499.7 17.4 all-reduce.5
